TPU v7x, 32 devices: a whole 2x2x4 slice. The times are simulated.
32 devices in a mesh: parts: 2 (over y), pol: 4 (over z), scen: 2 (over x), fund: 2 (over core).
Axes of the slice: x: 2, y: 2, z: 4, core: 2. Of those that a mesh axis runs over, the one named last changes fastest.
Arguments:
- count_init: float32 [32768], P(('pol', 'fund')), may hold values from 0.5 to 2
- value_init: float32 [32768], P(('pol', 'fund')), may hold values from 0.5 to 4
- durations: int32 [32768], P(('pol', 'fund')), may hold values from 0 to 119
- products: int32 [32768], P(('pol', 'fund')), may hold values from 0 to 7
- policy_fund: int32 [32768], P(('pol', 'fund')), may hold values from 0 to 119, as said below
- lapse_base: float32 [8], replicated, may hold values from 0.05 to 0.1
- lapse_sens: float32 [8], replicated, may hold values from 6 to 10
- fee_rate: float32 [8], replicated, may hold values from 0.002 to 0.02
- fund_share: float32 [120], replicated, may hold values from 0.3 to 1
- bond_flows: float32 [16384, 120], P(('pol', 'fund')), may hold values from 0.05 to 1
- bond_fund: int32 [16384], P(('pol', 'fund')), may hold values from 0 to 119, as said below
- holdings: float32 [16384], P(('pol', 'fund')), may hold values from 0.037 to 0.3
- scen_rates: float32 [3, 120, 512], P(None, None, ('parts', 'scen')), parts along dimension 2, may hold values from 0 to 0.12
Outputs:
- credited: float32 [3, 120, 512], P(None, None, ('parts', 'scen')), parts along dimension 2
- reserve: float32 [512, 32768], P(('parts', 'scen'), ('pol', 'fund')), parts along dimension 0
There are 2 independent parts, one for each index of `parts`. A program takes and returns all parts, laid end to end along the dimension named above; an argument that names none is the same for every part. Nothing has to cross between parts.
Inputs may be any that keep to these rules, and one draw needn't show every extreme that they name: `policy_fund`: every fund number appears at least once. `bond_fund`: every fund number appears at least once.
All inputs are finite; a program needn't handle non-finite values.
Results may differ from a plain program's by a relative error of at most 0.0003.
Values sent between devices are 32-bit elements; how exact they have to be, the bound alone decides.
A program may use at most 64 MiB of HBM per device.

v0:
```python
import math
import jax
import jax.numpy as jnp
from jax import lax
from jax.sharding import PartitionSpec as P

surrender_end = 84
highest = lax.Precision.HIGHEST
contract_cols = (((1,), (1,)), ((), ()))
contract_rows = (((0,), (0,)), ((), ()))


def onehot_cols(fund_ids, offset_at, breadth, fund_count):
    picked = lax.dynamic_slice_in_dim(fund_ids, offset_at, breadth, 0)
    return (lax.broadcasted_iota(jnp.int32, (fund_count, breadth), 0) == picked[None, :]).astype(
        jnp.float32
    )


def lookup(code_ids, values):
    kind_count = values.shape[0]
    matches = (
        lax.broadcasted_iota(jnp.int32, (kind_count, code_ids.shape[0]), 0) == code_ids[None, :]
    )
    return jnp.sum(jnp.where(matches, values[:, None], 0.0), axis=0)


def fund_totals(weights, fund_ids, fund_count, breadth):
    scen_rows, pol_count = weights.shape

    def add_block(block_idx, running):
        offset_at = block_idx * breadth
        onehot = onehot_cols(fund_ids, offset_at, breadth, fund_count)
        piece_blk = lax.dynamic_slice_in_dim(weights, offset_at, breadth, 1)
        return running + lax.dot_general(
            onehot, piece_blk, contract_cols, precision=highest, preferred_element_type=jnp.float32
        )

    return lax.fori_loop(
        0, pol_count // breadth, add_block, jnp.zeros((fund_count, scen_rows), jnp.float32)
    )


def advance(
    in_force,
    account,
    credited,
    market,
    lapse_pol,
    sens_pol,
    fee_pol,
    durations,
    fund_ids,
    month_idx,
    breadth,
    want_totals,
):
    fund_count = credited.shape[0]
    scen_rows, pol_count = in_force.shape

    def move_block(block_idx, carried):
        force_all, account_all, running = carried
        offset_at = block_idx * breadth
        onehot = onehot_cols(fund_ids, offset_at, breadth, fund_count)
        credit_pol = lax.dot_general(
            credited, onehot, contract_rows, precision=highest, preferred_element_type=jnp.float32
        )
        force_blk = lax.dynamic_slice_in_dim(force_all, offset_at, breadth, 1)
        account_blk = lax.dynamic_slice_in_dim(account_all, offset_at, breadth, 1)
        lapse_blk = lax.dynamic_slice_in_dim(lapse_pol, offset_at, breadth, 0)
        sens_blk = lax.dynamic_slice_in_dim(sens_pol, offset_at, breadth, 0)
        fee_blk = lax.dynamic_slice_in_dim(fee_pol, offset_at, breadth, 0)
        dur_blk = lax.dynamic_slice_in_dim(durations, offset_at, breadth, 0)
        later_mult = jnp.where(dur_blk + month_idx >= surrender_end, 2.0, 1.0)
        lapse_now = (lapse_blk * later_mult)[None, :] * jnp.exp(
            sens_blk[None, :] * (market[:, None] - credit_pol)
        )
        force_new = force_blk * jnp.exp(-lapse_now)
        account_new = account_blk * jnp.exp(credit_pol / 12.0 - fee_blk[None, :])
        force_all = lax.dynamic_update_slice_in_dim(force_all, force_new, offset_at, 1)
        account_all = lax.dynamic_update_slice_in_dim(account_all, account_new, offset_at, 1)
        if want_totals:
            running = running + lax.dot_general(
                onehot,
                force_new * account_new,
                contract_cols,
                precision=highest,
                preferred_element_type=jnp.float32,
            )
        return (force_all, account_all, running)

    return lax.fori_loop(
        0,
        pol_count // breadth,
        move_block,
        (in_force, account, jnp.zeros((fund_count, scen_rows), jnp.float32)),
    )


def local(
    count_init,
    value_init,
    durations,
    products,
    policy_fund,
    lapse_base,
    lapse_sens,
    fee_rate,
    fund_share,
    bond_flows,
    bond_fund,
    holdings,
    scen_rates,
):
    fund_count = fund_share.shape[0]
    months = scen_rates.shape[0]
    tenors = scen_rates.shape[1]
    scen_rows = scen_rates.shape[2]
    pol_count = count_init.shape[0]
    breadth = math.gcd(pol_count, 1024)
    tenor_years = (jnp.arange(tenors).astype(jnp.float32) + 1.0) / 12.0
    lapse_pol = lookup(products, lapse_base)
    sens_pol = lookup(products, lapse_sens)
    fee_pol = lookup(products, fee_rate)
    bond_onehot = onehot_cols(bond_fund, 0, bond_fund.shape[0], fund_count)

    def asset_part(month_num):
        discount = jnp.exp(-scen_rates[month_num] * tenor_years[:, None])
        bond_values = jnp.dot(
            bond_flows, discount, precision=highest, preferred_element_type=jnp.float32
        )
        return jnp.dot(
            bond_onehot,
            bond_values * holdings[:, None],
            precision=highest,
            preferred_element_type=jnp.float32,
        )

    asset_stack = lax.psum(
        jnp.stack([asset_part(month_num) for month_num in range(months)]), ("pol", "fund")
    )
    start_totals = fund_totals((count_init * value_init)[None, :], policy_fund, fund_count, breadth)
    liab_part = jnp.broadcast_to(start_totals, (fund_count, scen_rows))
    in_force = jnp.broadcast_to(count_init[None, :], (scen_rows, pol_count))
    account = jnp.broadcast_to(value_init[None, :], (scen_rows, pol_count))
    credited_list = []
    for month_idx in range(months):
        assets = asset_stack[month_idx]
        liabilities = lax.psum(liab_part, ("pol", "fund"))
        credited = fund_share[:, None] * jnp.log(assets / liabilities)
        market = scen_rates[month_idx, tenors - 1]
        in_force, account, liab_part = advance(
            in_force,
            account,
            credited,
            market,
            lapse_pol,
            sens_pol,
            fee_pol,
            durations,
            policy_fund,
            month_idx,
            breadth,
            month_idx < months - 1,
        )
        credited_list.append(credited)
    return (jnp.stack(credited_list), in_force * account)


def solution(mesh):
    in_specs = (
        P(("pol", "fund")),
        P(("pol", "fund")),
        P(("pol", "fund")),
        P(("pol", "fund")),
        P(("pol", "fund")),
        P(),
        P(),
        P(),
        P(),
        P(("pol", "fund"), None),
        P(("pol", "fund")),
        P(("pol", "fund")),
        P(None, None, ("parts", "scen")),
    )
    out_specs = (P(None, None, ("parts", "scen")), P(("parts", "scen"), ("pol", "fund")))
    return jax.shard_map(local, mesh=mesh, in_specs=in_specs, out_specs=out_specs, check_vma=False)
```

profile of v0, /device:TPU:0, one launch (start us, length us, event | category | flops | bytes accessed | tf_op | source)
XLA Modules:
  0.0 272.6 jit_solution(3409827075269828922)
XLA Ops:
  17.2 30.9 %psum.29 = f32[120,128]{1,0:T(8,128)S(1)} all-reduce(f32[120,128]{1,0:T(8,128)S(1)} %broadcast_in_dim.151), channel_id=1, replica_groups=mesh['parts'=2,'pol'=4,'scen'=2,'fund'=2] {'pol','fund'}, use_global_device_ids=true, to_apply=%region_3.4 | all-reduce | flops 15360 | bytes 122880 | tf_op jit(solution)/shard_map/psum | solution.py:149
  48.3 24.1 %all-reduce.2.cloned.1.call-done = f32[3,120,128]{2,1,0:T(8,128)} async-done(((f32[3,120,128]{2,1,0:T(8,128)}), f32[3,120,128]{2,1,0:T(8,128)}) %all-reduce.2.cloned.1.call-update) | async-done | bytes 184336 | tf_op jit(solution)/shard_map/psum | solution.py:139
  75.9 57.0 %while.67 = (s32[]{:T(128)}, f32[128,4096]{0,1:T(8,128)S(1)}, f32[128,4096]{0,1:T(8,128)}, f32[120,128]{1,0:T(8,128)S(1)}, f32[4096]{0:T(1024)S(1)}, /*index=5*/...) while((s32[]{:T(128)}, f32[128,4096]{0,1:T(8,128)S(1)}, ...), condition=%wide.region_8.9_spmd.clone, body=%wide.region_7.8_spmd.clone.sunk | while | flops 379995136 | bytes 21226716 | solution.py:92
  76.0 3.1 %copy.21 = f32[128,4096]{0,1:T(8,128)} copy(f32[128,4096]{0,1:T(8,128)} %get-tuple-element.1082) | data formatting | bytes 4194304 | tf_op jit(solution)/shard_map/while
  80.3 3.1 %constant_dynamic-update-slice_fusion.6 = (f32[128,4096]{0,1:T(8,128)}, f32[128,4096]{0,1:T(8,128)}, f32[1024,128]{1,0:T(8,128)}) fusion(f32[128,4096]{0,1:T(8,128)} %copy.21, s32[]{:T(128)S(6)} %select_n.110, f32[1024]{0:T(1024)S(1)} %dynamic_slice.256, f32[128,4096]{0,1:T(8,128)} %copy.22, f32[128]{0:T(128)S(1)} %bitcast.142, ...), kind=kOutput, calls=%fused_computation.27.clone.1 | convolution fusion | flops 189915136 | bytes 2699780 | tf_op jit(solution)/shard_map/while/body/eval_jaxpr/dot_general | solution.py:65
  90.2 3.1 %copy.21 = f32[128,4096]{0,1:T(8,128)} copy(f32[128,4096]{0,1:T(8,128)} %get-tuple-element.1082) | data formatting | bytes 4194304 | tf_op jit(solution)/shard_map/while
  94.6 3.2 %constant_dynamic-update-slice_fusion.6 = (f32[128,4096]{0,1:T(8,128)}, f32[128,4096]{0,1:T(8,128)}, f32[1024,128]{1,0:T(8,128)}) fusion(f32[128,4096]{0,1:T(8,128)} %copy.21, s32[]{:T(128)S(6)} %select_n.110, f32[1024]{0:T(1024)S(1)} %dynamic_slice.256, f32[128,4096]{0,1:T(8,128)} %copy.22, f32[128]{0:T(128)S(1)} %bitcast.142, ...), kind=kOutput, calls=%fused_computation.27.clone.1 | convolution fusion | flops 189915136 | bytes 2699780 | tf_op jit(solution)/shard_map/while/body/eval_jaxpr/dot_general | solution.py:65
  104.4 3.1 %copy.21 = f32[128,4096]{0,1:T(8,128)} copy(f32[128,4096]{0,1:T(8,128)} %get-tuple-element.1082) | data formatting | bytes 4194304 | tf_op jit(solution)/shard_map/while
  108.8 3.2 %constant_dynamic-update-slice_fusion.6 = (f32[128,4096]{0,1:T(8,128)}, f32[128,4096]{0,1:T(8,128)}, f32[1024,128]{1,0:T(8,128)}) fusion(f32[128,4096]{0,1:T(8,128)} %copy.21, s32[]{:T(128)S(6)} %select_n.110, f32[1024]{0:T(1024)S(1)} %dynamic_slice.256, f32[128,4096]{0,1:T(8,128)} %copy.22, f32[128]{0:T(128)S(1)} %bitcast.142, ...), kind=kOutput, calls=%fused_computation.27.clone.1 | convolution fusion | flops 189915136 | bytes 2699780 | tf_op jit(solution)/shard_map/while/body/eval_jaxpr/dot_general | solution.py:65
  118.7 3.1 %copy.21 = f32[128,4096]{0,1:T(8,128)} copy(f32[128,4096]{0,1:T(8,128)} %get-tuple-element.1082) | data formatting | bytes 4194304 | tf_op jit(solution)/shard_map/while
  123.1 3.2 %constant_dynamic-update-slice_fusion.6 = (f32[128,4096]{0,1:T(8,128)}, f32[128,4096]{0,1:T(8,128)}, f32[1024,128]{1,0:T(8,128)}) fusion(f32[128,4096]{0,1:T(8,128)} %copy.21, s32[]{:T(128)S(6)} %select_n.110, f32[1024]{0:T(1024)S(1)} %dynamic_slice.256, f32[128,4096]{0,1:T(8,128)} %copy.22, f32[128]{0:T(128)S(1)} %bitcast.142, ...), kind=kOutput, calls=%fused_computation.27.clone.1 | convolution fusion | flops 189915136 | bytes 2699780 | tf_op jit(solution)/shard_map/while/body/eval_jaxpr/dot_general | solution.py:65
  132.9 27.7 %psum.30 = f32[120,128]{1,0:T(8,128)S(1)} all-reduce(f32[120,128]{1,0:T(8,128)S(1)} %get-tuple-element.624), channel_id=1, replica_groups=mesh['parts'=2,'pol'=4,'scen'=2,'fund'=2] {'pol','fund'}, use_global_device_ids=true, to_apply=%region_9.10 | all-reduce | flops 15360 | bytes 122880 | tf_op jit(solution)/shard_map/psum | solution.py:149
  161.6 57.0 %while.68 = (s32[]{:T(128)}, f32[128,4096]{0,1:T(8,128)S(1)}, f32[128,4096]{0,1:T(8,128)}, f32[120,128]{1,0:T(8,128)S(1)}, f32[4096]{0:T(1024)S(1)}, /*index=5*/...) while((s32[]{:T(128)}, f32[128,4096]{0,1:T(8,128)S(1)}, ...), condition=%wide.region_11.12_spmd.clone, body=%wide.region_10.11_spmd.clone.sunk | while | flops 379996160 | bytes 21226716 | solution.py:92
  161.6 3.1 %copy.23 = f32[128,4096]{0,1:T(8,128)} copy(f32[128,4096]{0,1:T(8,128)} %get-tuple-element.1127) | data formatting | bytes 4194304 | tf_op jit(solution)/shard_map/while
  166.0 3.1 %constant_dynamic-update-slice_fusion.7 = (f32[128,4096]{0,1:T(8,128)}, f32[128,4096]{0,1:T(8,128)}, f32[1024,128]{1,0:T(8,128)}) fusion(f32[128,4096]{0,1:T(8,128)} %copy.23, s32[]{:T(128)S(6)} %select_n.112, f32[1024]{0:T(1024)S(1)} %dynamic_slice.264, f32[128,4096]{0,1:T(8,128)} %copy.24, f32[128]{0:T(128)S(1)} %bitcast.140, ...), kind=kOutput, calls=%fused_computation.39.clone.1 | convolution fusion | flops 189915136 | bytes 2699780 | tf_op jit(solution)/shard_map/while/body/eval_jaxpr/dot_general | solution.py:65
  175.9 3.1 %copy.23 = f32[128,4096]{0,1:T(8,128)} copy(f32[128,4096]{0,1:T(8,128)} %get-tuple-element.1127) | data formatting | bytes 4194304 | tf_op jit(solution)/shard_map/while
  180.2 3.2 %constant_dynamic-update-slice_fusion.7 = (f32[128,4096]{0,1:T(8,128)}, f32[128,4096]{0,1:T(8,128)}, f32[1024,128]{1,0:T(8,128)}) fusion(f32[128,4096]{0,1:T(8,128)} %copy.23, s32[]{:T(128)S(6)} %select_n.112, f32[1024]{0:T(1024)S(1)} %dynamic_slice.264, f32[128,4096]{0,1:T(8,128)} %copy.24, f32[128]{0:T(128)S(1)} %bitcast.140, ...), kind=kOutput, calls=%fused_computation.39.clone.1 | convolution fusion | flops 189915136 | bytes 2699780 | tf_op jit(solution)/shard_map/while/body/eval_jaxpr/dot_general | solution.py:65
  190.1 3.1 %copy.23 = f32[128,4096]{0,1:T(8,128)} copy(f32[128,4096]{0,1:T(8,128)} %get-tuple-element.1127) | data formatting | bytes 4194304 | tf_op jit(solution)/shard_map/while
  194.5 3.2 %constant_dynamic-update-slice_fusion.7 = (f32[128,4096]{0,1:T(8,128)}, f32[128,4096]{0,1:T(8,128)}, f32[1024,128]{1,0:T(8,128)}) fusion(f32[128,4096]{0,1:T(8,128)} %copy.23, s32[]{:T(128)S(6)} %select_n.112, f32[1024]{0:T(1024)S(1)} %dynamic_slice.264, f32[128,4096]{0,1:T(8,128)} %copy.24, f32[128]{0:T(128)S(1)} %bitcast.140, ...), kind=kOutput, calls=%fused_computation.39.clone.1 | convolution fusion | flops 189915136 | bytes 2699780 | tf_op jit(solution)/shard_map/while/body/eval_jaxpr/dot_general | solution.py:65
  204.3 3.1 %copy.23 = f32[128,4096]{0,1:T(8,128)} copy(f32[128,4096]{0,1:T(8,128)} %get-tuple-element.1127) | data formatting | bytes 4194304 | tf_op jit(solution)/shard_map/while
  208.7 3.2 %constant_dynamic-update-slice_fusion.7 = (f32[128,4096]{0,1:T(8,128)}, f32[128,4096]{0,1:T(8,128)}, f32[1024,128]{1,0:T(8,128)}) fusion(f32[128,4096]{0,1:T(8,128)} %copy.23, s32[]{:T(128)S(6)} %select_n.112, f32[1024]{0:T(1024)S(1)} %dynamic_slice.264, f32[128,4096]{0,1:T(8,128)} %copy.24, f32[128]{0:T(128)S(1)} %bitcast.140, ...), kind=kOutput, calls=%fused_computation.39.clone.1 | convolution fusion | flops 189915136 | bytes 2699780 | tf_op jit(solution)/shard_map/while/body/eval_jaxpr/dot_general | solution.py:65
  218.6 26.4 %psum.31 = f32[120,128]{1,0:T(8,128)S(1)} all-reduce(f32[120,128]{1,0:T(8,128)S(1)} %get-tuple-element.627), channel_id=1, replica_groups=mesh['parts'=2,'pol'=4,'scen'=2,'fund'=2] {'pol','fund'}, use_global_device_ids=true, to_apply=%region_12.13 | all-reduce | flops 15360 | bytes 122880 | tf_op jit(solution)/shard_map/psum | solution.py:149
  245.8 11.2 %while.65 = (s32[]{:T(128)}, f32[128,4096]{0,1:T(8,128)S(1)}, f32[128,4096]{0,1:T(8,128)}, f32[4096]{0:T(1024)S(1)}, s32[4096]{0:T(1024)S(1)}, /*index=5*/f32[40...) while((s32[]{:T(128)}, f32[128,4096]{0,1:T(8,128)S(1)}, ...), condition=%wide.region_14.15_spmd, body=%wide.region_13.14_spmd.sunk | while | flops 189919232 | bytes 2212551 | solution.py:92
  261.9 3.1 %mul.323 = f32[128,4096]{1,0:T(8,128)} multiply(f32[128,4096]{1,0:T(8,128)S(1)} %copy-done.1, f32[128,4096]{1,0:T(8,128)} %copy.18) | non-fusion elementwise | flops 524288 | bytes 6291456 | tf_op jit(solution)/shard_map/mul | solution.py:167
  (146 shorter events, 96.9 us)
Async XLA Ops:
  7.2 1.2 copy-start
  7.2 3.1 %copy-start.5 = (f32[2048]{0:T(1024)S(1)}, f32[2048]{0:T(1024)}, u32[]{:S(2)}) copy-start(f32[2048]{0:T(1024)} %param.32) | copy-start | bytes 24580
  7.2 3.1 %copy-start.4 = (f32[3,120,128]{2,1,0:T(8,128)S(1)}, f32[3,120,128]{2,1,0:T(8,128)}, u32[]{:S(2)}) copy-start(f32[3,120,128]{2,1,0:T(8,128)} %param.33) | copy-start | bytes 552964
  7.2 65.3 %all-reduce.2.cloned.1.call-start = ((), (), s32[]{:S(2)}) async-start(), calls=%async_computation | async-start | bytes 368640 | tf_op jit(solution)/shard_map/psum | solution.py:139
  10.3 2.2 copy-start.6
  12.6 3.1 %copy-start.7 = (f32[4096]{0:T(1024)S(1)}, f32[4096]{0:T(1024)}, u32[]{:S(2)}) copy-start(f32[4096]{0:T(1024)} %param.21) | copy-start | bytes 49156
  12.6 3.1 %copy-start.8 = (f32[4096]{0:T(1024)S(1)}, f32[4096]{0:T(1024)}, u32[]{:S(2)}) copy-start(f32[4096]{0:T(1024)} %param.22) | copy-start | bytes 49156
  12.6 3.1 %copy-start.2 = (s32[4096]{0:T(1024)S(1)}, s32[4096]{0:T(1024)}, u32[]{:S(2)}) copy-start(s32[4096]{0:T(1024)} %param.25) | copy-start | bytes 49156
  13.4 34.8 %copy-start.9 = (s32[4096]{0:T(1024)S(1)}, s32[4096]{0:T(1024)}, u32[]{:S(2)}) copy-start(s32[4096]{0:T(1024)} %param.24) | copy-start | bytes 49156
  13.4 34.7 %copy-start.11 = (f32[8]{0:T(128)S(1)}, f32[8]{0:T(128)}, u32[]{:S(2)}) copy-start(f32[8]{0:T(128)} %param.28) | copy-start | bytes 100
  13.4 34.7 %copy-start.12 = (f32[8]{0:T(128)S(1)}, f32[8]{0:T(128)}, u32[]{:S(2)}) copy-start(f32[8]{0:T(128)} %param.27) | copy-start | bytes 100
  13.4 34.7 %copy-start.13 = (f32[8]{0:T(128)S(1)}, f32[8]{0:T(128)}, u32[]{:S(2)}) copy-start(f32[8]{0:T(128)} %param.26) | copy-start | bytes 100
  13.4 59.0 %copy-start.10 = (f32[120]{0:T(128)S(1)}, f32[120]{0:T(128)}, u32[]{:S(2)}) copy-start(f32[120]{0:T(128)} %param.29) | copy-start | bytes 1444
  73.4 2.5 copy-start.3
  258.9 3.0 %copy-start.1 = (f32[128,4096]{1,0:T(8,128)S(1)}, f32[128,4096]{1,0:T(8,128)}, u32[]{:S(2)}) copy-start(f32[128,4096]{1,0:T(8,128)} %copy.17) | copy-start | bytes 6291460
Sparse Core Ops, SparseCore 0:
  15.8 56.6 all-reduce.1
where the time goes:
time: 274 us; the launch traced here: 273 us
  blocking collectives  85 us (31%)
  local copies, waits for them, and re-layouts  81 us (30%)
  matrix products  60 us (22%)
  waiting for transfers between devices  24.1 us (9%)
  between operations  14.4 us (5%)
  other arithmetic  7.53 us (3%)
    psum x3, blocking collectives, local(): liabilities = lax.psum(liab_part, ('pol', 'fund'))  85 us
    while x32, local copies, waits for them, and re-layouts  72 us
    dot_general x12, matrix products, move_block(): lax.dot_general(credited, onehot, contract_rows, precision=highest, prefe...  36.4 us
    psum x1, waiting for transfers between devices, local(): lax.psum(jnp.stack([asset_part(month_num) for month_num in range(months)]...  24.1 us
    dot_general x8, matrix products, move_block(): lax.dot_general(onehot, force_new * account_new, contract_cols, precision...  16.2 us
  transfers between devices with their start and end apart: 1, of which 1 were waited for; matrix products, arithmetic and copies ran while one was open for 1% of the time, Pallas kernels for 0%

commit v1 on v0

--- a/solution.py
+++ b/solution.py
@@ -146,7 +146,7 @@
     credited_list = []
     for month_idx in range(months):
         assets = asset_stack[month_idx]
-        liabilities = lax.psum(liab_part, ("pol", "fund"))
+        liabilities = lax.psum(lax.psum(liab_part, "fund"), "pol")
         credited = fund_share[:, None] * jnp.log(assets / liabilities)
         market = scen_rates[month_idx, tenors - 1]
         in_force, account, liab_part = advance(

time: 274 us -> 263 us (0.960)
  blocking collectives: 85 us -> 67.8 us
  waiting for transfers between devices: 24.1 us -> 30.2 us
    psum x3 -> x6, blocking collectives: 85 us -> 67.8 us  [local(): liabilities = lax.psum(lax.psum(liab_part, 'fund'), 'pol')]
    psum x1, waiting for transfers between devices: 24.1 us -> 30.2 us  [local(): lax.psum(jnp.stack([asset_part(month_num) for month_num in range(months)]...]
where the time goes in v1:
time: 263 us; the launch traced here: 262 us
  local copies, waits for them, and re-layouts  81.1 us (31%)
  blocking collectives  67.8 us (26%)
  matrix products  60 us (23%)
  waiting for transfers between devices  30.2 us (11%)
  between operations  14.4 us (5%)
  other arithmetic  7.57 us (3%)
    while x32, local copies, waits for them, and re-layouts  72.1 us
    psum x6, blocking collectives, local(): liabilities = lax.psum(lax.psum(liab_part, 'fund'), 'pol')  67.8 us
    dot_general x12, matrix products, move_block(): lax.dot_general(credited, onehot, contract_rows, precision=highest, prefe...  36.4 us
    psum x1, waiting for transfers between devices, local(): lax.psum(jnp.stack([asset_part(month_num) for month_num in range(months)]...  30.2 us
    dot_general x8, matrix products, move_block(): lax.dot_general(onehot, force_new * account_new, contract_cols, precision...  16.2 us
  transfers between devices with their start and end apart: 1, of which 1 were waited for; matrix products, arithmetic and copies ran while one was open for 1% of the time, Pallas kernels for 0%

profile of v1, /device:TPU:0, one launch (start us, length us, event | category | flops | bytes accessed | tf_op | source)
XLA Modules:
  0.0 261.7 jit_solution(2698670872480252246)
XLA Ops:
  17.2 3.9 %psum.50 = f32[120,128]{1,0:T(8,128)S(1)} all-reduce(f32[120,128]{1,0:T(8,128)S(1)} %broadcast_in_dim.151), channel_id=1, replica_groups=mesh['parts'=2,'pol'=4,'scen'=2,'fund'=2] {'fund'}, use_global_device_ids=true, to_apply=%region_3.4 | all-reduce | flops 15360 | bytes 122880 | tf_op jit(solution)/shard_map/psum | solution.py:149
  21.2 21.1 %psum.51 = f32[120,128]{1,0:T(8,128)S(1)} all-reduce(f32[120,128]{1,0:T(8,128)S(1)} %psum.50), channel_id=1, replica_groups=mesh['parts'=2,'pol'=4,'scen'=2,'fund'=2] {'pol'}, use_global_device_ids=true, to_apply=%region_4.5 | all-reduce | flops 15360 | bytes 122880 | tf_op jit(solution)/shard_map/psum | solution.py:149
  42.5 30.2 %all-reduce.2.cloned.1.call-done = f32[3,120,128]{2,1,0:T(8,128)} async-done(((f32[3,120,128]{2,1,0:T(8,128)}), f32[3,120,128]{2,1,0:T(8,128)}) %all-reduce.2.cloned.1.call-update) | async-done | bytes 184336 | tf_op jit(solution)/shard_map/psum | solution.py:139
  76.2 57.0 %while.67 = (s32[]{:T(128)}, f32[128,4096]{0,1:T(8,128)S(1)}, f32[128,4096]{0,1:T(8,128)}, f32[120,128]{1,0:T(8,128)S(1)}, f32[4096]{0:T(1024)S(1)}, /*index=5*/...) while((s32[]{:T(128)}, f32[128,4096]{0,1:T(8,128)S(1)}, ...), condition=%wide.region_9.10_spmd.clone, body=%wide.region_8.9_spmd.clone.sunk | while | flops 379995136 | bytes 21226716 | solution.py:92
  76.3 3.1 %copy.21 = f32[128,4096]{0,1:T(8,128)} copy(f32[128,4096]{0,1:T(8,128)} %get-tuple-element.1082) | data formatting | bytes 4194304 | tf_op jit(solution)/shard_map/while
  80.7 3.1 %constant_dynamic-update-slice_fusion.6 = (f32[128,4096]{0,1:T(8,128)}, f32[128,4096]{0,1:T(8,128)}, f32[1024,128]{1,0:T(8,128)}) fusion(f32[128,4096]{0,1:T(8,128)} %copy.21, s32[]{:T(128)S(6)} %select_n.110, f32[1024]{0:T(1024)S(1)} %dynamic_slice.256, f32[128,4096]{0,1:T(8,128)} %copy.22, f32[128]{0:T(128)S(1)} %bitcast.142, ...), kind=kOutput, calls=%fused_computation.27.clone.1 | convolution fusion | flops 189915136 | bytes 2699780 | tf_op jit(solution)/shard_map/while/body/eval_jaxpr/dot_general | solution.py:65
  90.5 3.1 %copy.21 = f32[128,4096]{0,1:T(8,128)} copy(f32[128,4096]{0,1:T(8,128)} %get-tuple-element.1082) | data formatting | bytes 4194304 | tf_op jit(solution)/shard_map/while
  94.9 3.2 %constant_dynamic-update-slice_fusion.6 = (f32[128,4096]{0,1:T(8,128)}, f32[128,4096]{0,1:T(8,128)}, f32[1024,128]{1,0:T(8,128)}) fusion(f32[128,4096]{0,1:T(8,128)} %copy.21, s32[]{:T(128)S(6)} %select_n.110, f32[1024]{0:T(1024)S(1)} %dynamic_slice.256, f32[128,4096]{0,1:T(8,128)} %copy.22, f32[128]{0:T(128)S(1)} %bitcast.142, ...), kind=kOutput, calls=%fused_computation.27.clone.1 | convolution fusion | flops 189915136 | bytes 2699780 | tf_op jit(solution)/shard_map/while/body/eval_jaxpr/dot_general | solution.py:65
  104.7 3.1 %copy.21 = f32[128,4096]{0,1:T(8,128)} copy(f32[128,4096]{0,1:T(8,128)} %get-tuple-element.1082) | data formatting | bytes 4194304 | tf_op jit(solution)/shard_map/while
  109.1 3.2 %constant_dynamic-update-slice_fusion.6 = (f32[128,4096]{0,1:T(8,128)}, f32[128,4096]{0,1:T(8,128)}, f32[1024,128]{1,0:T(8,128)}) fusion(f32[128,4096]{0,1:T(8,128)} %copy.21, s32[]{:T(128)S(6)} %select_n.110, f32[1024]{0:T(1024)S(1)} %dynamic_slice.256, f32[128,4096]{0,1:T(8,128)} %copy.22, f32[128]{0:T(128)S(1)} %bitcast.142, ...), kind=kOutput, calls=%fused_computation.27.clone.1 | convolution fusion | flops 189915136 | bytes 2699780 | tf_op jit(solution)/shard_map/while/body/eval_jaxpr/dot_general | solution.py:65
  119.0 3.1 %copy.21 = f32[128,4096]{0,1:T(8,128)} copy(f32[128,4096]{0,1:T(8,128)} %get-tuple-element.1082) | data formatting | bytes 4194304 | tf_op jit(solution)/shard_map/while
  123.4 3.2 %constant_dynamic-update-slice_fusion.6 = (f32[128,4096]{0,1:T(8,128)}, f32[128,4096]{0,1:T(8,128)}, f32[1024,128]{1,0:T(8,128)}) fusion(f32[128,4096]{0,1:T(8,128)} %copy.21, s32[]{:T(128)S(6)} %select_n.110, f32[1024]{0:T(1024)S(1)} %dynamic_slice.256, f32[128,4096]{0,1:T(8,128)} %copy.22, f32[128]{0:T(128)S(1)} %bitcast.142, ...), kind=kOutput, calls=%fused_computation.27.clone.1 | convolution fusion | flops 189915136 | bytes 2699780 | tf_op jit(solution)/shard_map/while/body/eval_jaxpr/dot_general | solution.py:65
  133.2 3.6 %psum.52 = f32[120,128]{1,0:T(8,128)S(1)} all-reduce(f32[120,128]{1,0:T(8,128)S(1)} %get-tuple-element.624), channel_id=1, replica_groups=mesh['parts'=2,'pol'=4,'scen'=2,'fund'=2] {'fund'}, use_global_device_ids=true, to_apply=%region_10.11 | all-reduce | flops 15360 | bytes 122880 | tf_op jit(solution)/shard_map/psum | solution.py:149
  136.8 19.2 %psum.53 = f32[120,128]{1,0:T(8,128)S(1)} all-reduce(f32[120,128]{1,0:T(8,128)S(1)} %psum.52), channel_id=1, replica_groups=mesh['parts'=2,'pol'=4,'scen'=2,'fund'=2] {'pol'}, use_global_device_ids=true, to_apply=%region_11.12 | all-reduce | flops 15360 | bytes 122880 | tf_op jit(solution)/shard_map/psum | solution.py:149
  156.9 57.0 %while.68 = (s32[]{:T(128)}, f32[128,4096]{0,1:T(8,128)S(1)}, f32[128,4096]{0,1:T(8,128)}, f32[120,128]{1,0:T(8,128)S(1)}, f32[4096]{0:T(1024)S(1)}, /*index=5*/...) while((s32[]{:T(128)}, f32[128,4096]{0,1:T(8,128)S(1)}, ...), condition=%wide.region_13.14_spmd.clone, body=%wide.region_12.13_spmd.clone.sunk | while | flops 379996160 | bytes 21226716 | solution.py:92
  157.0 3.1 %copy.23 = f32[128,4096]{0,1:T(8,128)} copy(f32[128,4096]{0,1:T(8,128)} %get-tuple-element.1127) | data formatting | bytes 4194304 | tf_op jit(solution)/shard_map/while
  161.4 3.1 %constant_dynamic-update-slice_fusion.7 = (f32[128,4096]{0,1:T(8,128)}, f32[128,4096]{0,1:T(8,128)}, f32[1024,128]{1,0:T(8,128)}) fusion(f32[128,4096]{0,1:T(8,128)} %copy.23, s32[]{:T(128)S(6)} %select_n.112, f32[1024]{0:T(1024)S(1)} %dynamic_slice.264, f32[128,4096]{0,1:T(8,128)} %copy.24, f32[128]{0:T(128)S(1)} %bitcast.140, ...), kind=kOutput, calls=%fused_computation.39.clone.1 | convolution fusion | flops 189915136 | bytes 2699780 | tf_op jit(solution)/shard_map/while/body/eval_jaxpr/dot_general | solution.py:65
  175.6 3.2 %constant_dynamic-update-slice_fusion.7 = (f32[128,4096]{0,1:T(8,128)}, f32[128,4096]{0,1:T(8,128)}, f32[1024,128]{1,0:T(8,128)}) fusion(f32[128,4096]{0,1:T(8,128)} %copy.23, s32[]{:T(128)S(6)} %select_n.112, f32[1024]{0:T(1024)S(1)} %dynamic_slice.264, f32[128,4096]{0,1:T(8,128)} %copy.24, f32[128]{0:T(128)S(1)} %bitcast.140, ...), kind=kOutput, calls=%fused_computation.39.clone.1 | convolution fusion | flops 189915136 | bytes 2699780 | tf_op jit(solution)/shard_map/while/body/eval_jaxpr/dot_general | solution.py:65
  189.8 3.2 %constant_dynamic-update-slice_fusion.7 = (f32[128,4096]{0,1:T(8,128)}, f32[128,4096]{0,1:T(8,128)}, f32[1024,128]{1,0:T(8,128)}) fusion(f32[128,4096]{0,1:T(8,128)} %copy.23, s32[]{:T(128)S(6)} %select_n.112, f32[1024]{0:T(1024)S(1)} %dynamic_slice.264, f32[128,4096]{0,1:T(8,128)} %copy.24, f32[128]{0:T(128)S(1)} %bitcast.140, ...), kind=kOutput, calls=%fused_computation.39.clone.1 | convolution fusion | flops 189915136 | bytes 2699780 | tf_op jit(solution)/shard_map/while/body/eval_jaxpr/dot_general | solution.py:65
  204.1 3.2 %constant_dynamic-update-slice_fusion.7 = (f32[128,4096]{0,1:T(8,128)}, f32[128,4096]{0,1:T(8,128)}, f32[1024,128]{1,0:T(8,128)}) fusion(f32[128,4096]{0,1:T(8,128)} %copy.23, s32[]{:T(128)S(6)} %select_n.112, f32[1024]{0:T(1024)S(1)} %dynamic_slice.264, f32[128,4096]{0,1:T(8,128)} %copy.24, f32[128]{0:T(128)S(1)} %bitcast.140, ...), kind=kOutput, calls=%fused_computation.39.clone.1 | convolution fusion | flops 189915136 | bytes 2699780 | tf_op jit(solution)/shard_map/while/body/eval_jaxpr/dot_general | solution.py:65
  214.0 3.6 %psum.54 = f32[120,128]{1,0:T(8,128)S(1)} all-reduce(f32[120,128]{1,0:T(8,128)S(1)} %get-tuple-element.627), channel_id=1, replica_groups=mesh['parts'=2,'pol'=4,'scen'=2,'fund'=2] {'fund'}, use_global_device_ids=true, to_apply=%region_14.15 | all-reduce | flops 15360 | bytes 122880 | tf_op jit(solution)/shard_map/psum | solution.py:149
  217.5 16.4 %psum.55 = f32[120,128]{1,0:T(8,128)S(1)} all-reduce(f32[120,128]{1,0:T(8,128)S(1)} %psum.54), channel_id=1, replica_groups=mesh['parts'=2,'pol'=4,'scen'=2,'fund'=2] {'pol'}, use_global_device_ids=true, to_apply=%region_15.16 | all-reduce | flops 15360 | bytes 122880 | tf_op jit(solution)/shard_map/psum | solution.py:149
  234.9 11.2 %while.65 = (s32[]{:T(128)}, f32[128,4096]{0,1:T(8,128)S(1)}, f32[128,4096]{0,1:T(8,128)}, f32[4096]{0:T(1024)S(1)}, s32[4096]{0:T(1024)S(1)}, /*index=5*/f32[40...) while((s32[]{:T(128)}, f32[128,4096]{0,1:T(8,128)S(1)}, ...), condition=%wide.region_17.18_spmd, body=%wide.region_16.17_spmd.sunk | while | flops 189919232 | bytes 2212551 | solution.py:92
  251.0 3.2 %mul.323 = f32[128,4096]{1,0:T(8,128)} multiply(f32[128,4096]{1,0:T(8,128)S(1)} %copy-done.1, f32[128,4096]{1,0:T(8,128)} %copy.18) | non-fusion elementwise | flops 524288 | bytes 6291456 | tf_op jit(solution)/shard_map/mul | solution.py:167
  (149 shorter events, 106.1 us)
Async XLA Ops:
  7.2 1.2 copy-start
  7.2 3.1 %copy-start.5 = (f32[2048]{0:T(1024)S(1)}, f32[2048]{0:T(1024)}, u32[]{:S(2)}) copy-start(f32[2048]{0:T(1024)} %param.32) | copy-start | bytes 24580
  7.2 3.1 %copy-start.4 = (f32[3,120,128]{2,1,0:T(8,128)S(1)}, f32[3,120,128]{2,1,0:T(8,128)}, u32[]{:S(2)}) copy-start(f32[3,120,128]{2,1,0:T(8,128)} %param.33) | copy-start | bytes 552964
  7.2 65.6 %all-reduce.2.cloned.1.call-start = ((), (), s32[]{:S(2)}) async-start(), calls=%async_computation | async-start | bytes 368640 | tf_op jit(solution)/shard_map/psum | solution.py:139
  10.3 2.2 copy-start.6
  12.6 3.1 %copy-start.7 = (f32[4096]{0:T(1024)S(1)}, f32[4096]{0:T(1024)}, u32[]{:S(2)}) copy-start(f32[4096]{0:T(1024)} %param.21) | copy-start | bytes 49156
  12.6 3.1 %copy-start.8 = (f32[4096]{0:T(1024)S(1)}, f32[4096]{0:T(1024)}, u32[]{:S(2)}) copy-start(f32[4096]{0:T(1024)} %param.22) | copy-start | bytes 49156
  12.6 3.1 %copy-start.2 = (s32[4096]{0:T(1024)S(1)}, s32[4096]{0:T(1024)}, u32[]{:S(2)}) copy-start(s32[4096]{0:T(1024)} %param.25) | copy-start | bytes 49156
  13.4 29.0 %copy-start.9 = (s32[4096]{0:T(1024)S(1)}, s32[4096]{0:T(1024)}, u32[]{:S(2)}) copy-start(s32[4096]{0:T(1024)} %param.24) | copy-start | bytes 49156
  13.4 28.9 %copy-start.11 = (f32[8]{0:T(128)S(1)}, f32[8]{0:T(128)}, u32[]{:S(2)}) copy-start(f32[8]{0:T(128)} %param.28) | copy-start | bytes 100
  13.4 28.9 %copy-start.12 = (f32[8]{0:T(128)S(1)}, f32[8]{0:T(128)}, u32[]{:S(2)}) copy-start(f32[8]{0:T(128)} %param.27) | copy-start | bytes 100
  13.4 28.9 %copy-start.13 = (f32[8]{0:T(128)S(1)}, f32[8]{0:T(128)}, u32[]{:S(2)}) copy-start(f32[8]{0:T(128)} %param.26) | copy-start | bytes 100
  13.4 59.4 %copy-start.10 = (f32[120]{0:T(128)S(1)}, f32[120]{0:T(128)}, u32[]{:S(2)}) copy-start(f32[120]{0:T(128)} %param.29) | copy-start | bytes 1444
  73.7 2.5 copy-start.3
  247.9 3.0 %copy-start.1 = (f32[128,4096]{1,0:T(8,128)S(1)}, f32[128,4096]{1,0:T(8,128)}, u32[]{:S(2)}) copy-start(f32[128,4096]{1,0:T(8,128)} %copy.17) | copy-start | bytes 6291460
Sparse Core Ops, SparseCore 0:
  15.8 56.9 all-reduce.1
